TPU v7x, 512 devices: a whole 4x8x8 slice. The times are simulated.
512 devices in a mesh: fsdp: 16 (over y, x_lo), ed: 32 (over x_hi, z, core).
Axes of the slice: x: 4 (x_hi: 2, x_lo: 2; x = x_hi * 2 + x_lo), y: 8, z: 8, core: 2. Of those that a mesh axis runs over, the one named last changes fastest.
Arguments:
- tokens: bfloat16 [9216, 6144], P('ed', 'fsdp'), may hold values from -6 to 6
- expert_ids: int32 [9216, 2], P('ed'), may hold values from 0 to 7, all different within a row; in each aligned block of 288 rows (0 to 287, 288 to 575, ...) at most 81 rows name the same one
- route_weights: float32 [9216, 2], P('ed'), may hold values from 0.1 to 1
- w_gate: bfloat16 [1, 6144, 8192], P(None, 'fsdp', 'ed'), may hold values from -0.078125 to 0.078125
- w_up: bfloat16 [1, 6144, 8192], P(None, 'fsdp', 'ed'), may hold values from -0.078125 to 0.078125
- w_down: bfloat16 [1, 8192, 6144], P(None, 'ed', 'fsdp'), may hold values from -0.0625 to 0.0625
Outputs:
- mixed: bfloat16 [9216, 6144], P('ed', 'fsdp')
Inputs may be any that keep to these rules, and one draw needn't show every extreme that they name: `expert_ids`: each row names two different experts. In each block of 288 rows that one index of ed holds, no expert is named by more than 81 rows, a bound that some block reaches.
All inputs are finite; a program needn't handle non-finite values.
Results may differ from a plain program's by a relative error of at most 0.025.
Values may be sent and summed in bfloat16 or wider, within the bound.
A program may use at most 64 MiB of HBM per device.

v0:
```python
import jax
import jax.numpy as jnp
from jax import lax
from jax.sharding import PartitionSpec as P

CAP = 81


def slot_match(routes, window, capacity):
    window_ids = jnp.arange(window, dtype=jnp.int32)
    routed = jnp.any(routes[:, :, None, :] == window_ids[None, None, :, None], axis=3)
    position = jnp.cumsum(routed.astype(jnp.int32), axis=1) - 1
    slot_ids = jnp.arange(capacity, dtype=jnp.int32)
    hits = routed[:, :, :, None] & (position[:, :, :, None] == slot_ids[None, None, None, :])
    return hits.astype(jnp.int32)


def take_block(block_rows, row_list):
    return jnp.take(block_rows, row_list, axis=0)


def pick_rows(blocks, routes, window, capacity):
    match = slot_match(routes, window, capacity)
    row_numbers = jnp.arange(blocks.shape[1], dtype=jnp.int32)
    source_row = jnp.sum(match * row_numbers[None, :, None, None], axis=1).reshape(
        blocks.shape[0], window * capacity
    )
    filled = jnp.sum(match, axis=1).reshape(blocks.shape[0], window * capacity)
    picked = jax.vmap(take_block)(blocks, source_row)
    picked = jnp.where(filled[:, :, None] > 0, picked, jnp.zeros_like(picked))
    return picked.reshape(blocks.shape[0], window, capacity, blocks.shape[2])


def combine_matrix(routes, weights, window, capacity):
    match = slot_match(routes[None], window, capacity)[0]
    window_ids = jnp.arange(window, dtype=jnp.int32)
    per_expert = jnp.sum(
        jnp.where(
            routes[:, None, :] == window_ids[None, :, None],
            weights[:, None, :],
            jnp.zeros_like(weights[:, None, :]),
        ),
        axis=2,
    )
    return (per_expert[:, :, None] * match.astype(weights.dtype)).reshape(
        routes.shape[0], window * capacity
    )


def local(tokens, expert_ids, route_weights, w_gate, w_up, w_down):
    window = w_gate.shape[0]
    features_dev = tokens.shape[1]
    own_slots = pick_rows(tokens[None], expert_ids[None], window, CAP)[0]
    selected = lax.all_gather(own_slots, "ed", axis=1, tiled=True)
    rows_full = lax.all_to_all(selected, "fsdp", split_axis=1, concat_axis=2, tiled=True)
    gate_part = jnp.einsum(
        "hnm,hmq->hnq",
        rows_full,
        lax.all_gather(w_gate, "fsdp", axis=1, tiled=True),
        preferred_element_type=jnp.float32,
    )
    up_part = jnp.einsum(
        "hnm,hmq->hnq",
        rows_full,
        lax.all_gather(w_up, "fsdp", axis=1, tiled=True),
        preferred_element_type=jnp.float32,
    )
    activation = (jax.nn.silu(gate_part) * up_part).astype(jnp.bfloat16)
    act_one = activation[0]

    def columns_out(shard_piece, first_col, act_one=act_one):
        return jnp.dot(act_one, shard_piece, preferred_element_type=jnp.float32)

    whole_rows = columns_out(lax.all_gather(w_down[0], "fsdp", axis=1, tiled=True), jnp.int32(0))
    outputs_list = [whole_rows.astype(jnp.bfloat16)]
    stacked = jnp.stack(outputs_list)
    exchanged = lax.all_to_all(stacked, "fsdp", split_axis=2, concat_axis=1, tiled=True)
    partial_out = exchanged.astype(jnp.float32)
    slot_out = lax.psum_scatter(
        partial_out.astype(jnp.bfloat16), "ed", scatter_dimension=1, tiled=True
    ).astype(jnp.float32)
    weights_matrix = combine_matrix(expert_ids, route_weights, window, CAP)
    mixed = jnp.dot(
        weights_matrix,
        slot_out.reshape(window * CAP, features_dev),
        precision=lax.Precision.HIGHEST,
        preferred_element_type=jnp.float32,
    )
    return mixed.astype(jnp.bfloat16)


def solution(mesh):
    return jax.shard_map(
        local,
        mesh=mesh,
        in_specs=(
            P("ed", "fsdp"),
            P("ed", None),
            P("ed", None),
            P(None, "fsdp", "ed"),
            P(None, "fsdp", "ed"),
            P(None, "ed", "fsdp"),
        ),
        out_specs=P("ed", "fsdp"),
        check_vma=False,
    )
```

profile of v0, /device:TPU:1, one launch (start us, length us, event | category | flops | bytes accessed | tf_op | source)
XLA Modules:
  0.0 640.9 jit_solution(6663339600788899471)
XLA Ops:
  8.1 3.0 convert_reduce_fusion
  11.1 1.3 gather_fusion
  12.5 0.7 copy.18
  15.4 96.3 %all-gather.6.cloned.1.call-done = bf16[1,2592,384]{2,0,1:T(2,128)(2,1)} async-done(((bf16[1,81,384]{2,0,1:T(2,128)(2,1)}), bf16[1,2592,384]{2,0,1:T(2,128)(2,1)}) %all-gather.6.cloned.1.call-update) | async-done | bytes 1990672 | tf_op jit(solution)/shard_map/all_gather | solution.py:54
  112.2 15.8 %reduce.14 = bf16[2592,384]{1,0:T(8,128)(2,1)S(1)} reduce(bf16[2592,1,384]{2,1,0:T(2,128)(2,1)} %bitcast.80, bf16[]{:T(256)} %broadcast.283), dimensions={1}, to_apply=%bitcast.61.reduce_sub_computation | reduce | bytes 3981314
  128.0 1.6 reshape.463
  129.6 71.7 %all_to_all.33 = bf16[16,2,31104]{2,1,0:T(2,128)(2,1)S(1)} all-to-all(bf16[16,2,31104]{2,1,0:T(2,128)(2,1)} %reshape.463), channel_id=1, replica_groups=mesh['fsdp'=16,'ed'=32] {'fsdp'}, dimensions={0} | all-to-all | bytes 3981312 | tf_op jit(solution)/shard_map/all_to_all | solution.py:55
  201.2 8.9 %reshape.464 = bf16[2592,1,384]{2,1,0:T(2,128)(2,1)} reshape(bf16[16,2,31104]{2,1,0:T(2,128)(2,1)S(1)} %all_to_all.33) | data formatting | bytes 3981312
  210.2 17.6 %bitcast_reduce_fusion = bf16[2592,384]{1,0:T(8,128)(2,1)} fusion(bf16[2592,1,384]{2,1,0:T(2,128)(2,1)} %reshape.464), kind=kLoop, calls=%fused_computation.46 | loop fusion | bytes 3981312 | tf_op jit(solution)/shard_map/all_to_all | solution.py:55
  227.8 1.8 all_to_all.25
  230.6 2.7 fusion.5
  233.3 66.1 %all-gather.10.cloned.1.call-done = bf16[1,6144,256]{2,1,0:T(8,128)(2,1)} async-done(((bf16[1,384,256]{2,1,0:T(8,128)(2,1)}), bf16[1,6144,256]{2,1,0:T(8,128)(2,1)}) %all-gather.10.cloned.1.call-update) | async-done | bytes 3145744 | tf_op jit(solution)/shard_map/all_gather | solution.py:65
  299.3 85.3 %all-gather.12.cloned.1.call-done = bf16[1,256,6144]{2,1,0:T(8,128)(2,1)} async-done(((bf16[1,256,384]{2,1,0:T(8,128)(2,1)}), bf16[1,256,6144]{2,1,0:T(8,128)(2,1)}) %all-gather.12.cloned.1.call-update) | async-done | bytes 3145744 | tf_op jit(solution)/shard_map/all_gather | solution.py:74
  384.6 6.5 %fusion.1 = bf16[1,162,6144]{2,1,0:T(8,128)(2,1)} fusion(bf16[1,256,6144]{2,1,0:T(8,128)(2,1)} %all-gather.12.cloned.1.call-done, bf16[162,6144]{1,0:T(8,128)(2,1)S(1)} %bitcast.74, bf16[1,6144,256]{2,1,0:T(8,128)(2,1)} %all-gather.10.cloned.1.call-done, f32[162,256]{1,0:T(8,128)S(1)} %fusion.5), kind=kOutput, calls=%fused_computation.2 | convolution fusion | flops 1020460032 | bytes 10438656 | tf_op jit(solution)/shard_map/dot_general | solution.py:72
  391.1 13.7 %copy.20 = bf16[1,162,6144]{1,0,2:T(2,128)(2,1)} copy(bf16[1,162,6144]{2,1,0:T(8,128)(2,1)} %fusion.1) | data formatting | bytes 3981312 | tf_op jit(solution)/shard_map/stack | solution.py:76
  404.8 34.6 %reduce.15 = bf16[6144,162]{1,0:T(8,128)(2,1)S(1)} reduce(bf16[6144,1,162]{2,1,0:T(2,128)(2,1)} %bitcast.71, bf16[]{:T(256)} %broadcast.283), dimensions={1}, to_apply=%bitcast.63.reduce_sub_computation | reduce | bytes 3981314
  439.4 6.9 %reshape.465 = bf16[16,2,31104]{2,1,0:T(2,128)(2,1)} reshape(bf16[6144,162]{1,0:T(8,128)(2,1)S(1)} %reduce.15) | data formatting | bytes 3981312
  446.4 4.2 all-to-all-start.1
  450.7 42.9 %all-to-all-done.1 = bf16[16,2,31104]{2,1,0:T(2,128)(2,1)S(1)} async-done(((bf16[16,2,31104]{2,1,0:T(2,128)(2,1)}), bf16[16,2,31104]{2,1,0:T(2,128)(2,1)S(1)}, u32[]{:S(2)}, u32[]{:S(2)}) %all-to-all-start.1) | async-done | bytes 1990688 | tf_op jit(solution)/shard_map/all_to_all | solution.py:77
  493.5 12.1 %reshape.466 = bf16[6144,1,162]{2,1,0:T(2,128)(2,1)} reshape(bf16[16,2,31104]{2,1,0:T(2,128)(2,1)S(1)} %all-to-all-done.1) | data formatting | bytes 3981312
  505.6 13.8 %copy.21 = bf16[1,162,6144]{2,1,0:T(8,128)(2,1)S(1)} copy(bf16[1,162,6144]{1,0,2:T(2,128)(2,1)} %bitcast.72) | data formatting | bytes 3981312 | tf_op jit(solution)/shard_map/all_to_all | solution.py:77
  520.5 1.6 all_to_all.30
  522.0 81.8 %fusion = bf16[96,384]{1,0:T(8,128)(2,1)S(1)} fusion(bf16[1,2592,384]{2,1,0:T(8,128)(2,1)} %all_to_all.30), kind=kCustom, calls=%all-reduce-scatter | all-reduce-scatter fusion | flops 1179649 | bytes 2066432
  603.9 3.5 collective-permute-start
  607.5 1.3 collective-permute-start.1
  608.8 1.3 collective-permute-start.2
  610.1 1.3 collective-permute-start.3
  611.4 16.7 %collective-permute-start.4 = (bf16[81,384]{1,0:T(8,128)(2,1)S(1)}, bf16[81,384]{1,0:T(8,128)(2,1)S(1)}, u32[]{:S(2)}, u32[]{:S(2)}) collective-permute-start(bf16[81,384]{1,0:T(8,128)(2,1)S(1)} %slice.16), channel_id=1, source_target_pairs={{0,5},{1,6},{2,7},{3,8},{4,9},{5,10},{6,11},{7,12},{8,13},{9,14},{... | collective-permute-start | bytes 186632
  628.1 1.7 convert_multiply_fusion
  629.8 1.3 dynamic-slice.4
  631.8 1.6 concatenate.3
  633.4 1.0 convolution_convert_fusion.1
  (47 shorter events, 6.4 us)
Async XLA Ops:
  6.5 4.6 copy-start
  6.5 105.1 %all-gather.6.cloned.1.call-start = ((), (), s32[]{:S(2)}) async-start(), calls=%async_computation.2 | async-start | bytes 4105728 | tf_op jit(solution)/shard_map/all_gather | solution.py:54
  13.3 217.3 %all-gather.8.cloned.1.call-start = ((), (), s32[]{:S(2)}) async-start(), calls=%async_computation.3 | async-start | bytes 3342336 | tf_op jit(solution)/shard_map/all_gather | solution.py:59
  14.1 285.3 %all-gather.10.cloned.1.call-start = ((), (), s32[]{:S(2)}) async-start(), calls=%async_computation.4 | async-start | bytes 3342336 | tf_op jit(solution)/shard_map/all_gather | solution.py:65
  14.8 369.8 %all-gather.12.cloned.1.call-start = ((), (), s32[]{:S(2)}) async-start(), calls=%async_computation.5 | async-start | bytes 3342336 | tf_op jit(solution)/shard_map/all_gather | solution.py:74
  446.4 4.2 copy-start.2
  446.4 4.3 copy-start.3
  446.4 47.1 %all-to-all-start.1 = ((bf16[16,2,31104]{2,1,0:T(2,128)(2,1)}), bf16[16,2,31104]{2,1,0:T(2,128)(2,1)S(1)}, u32[]{:S(2)}, u32[]{:S(2)}) async-start(bf16[16,2,31104]{2,1,0:T(2,128)(2,1)} %reshape.465), calls=%async_computation.1 | async-start | bytes 3981312 | tf_op jit(solution)/shard_map/all_to_all | solution.py:77
  520.5 113.9 %copy-start.1 = (bf16[288,384]{1,0:T(8,128)(2,1)S(1)}, bf16[288,384]{1,0:T(8,128)(2,1)}, u32[]{:S(2)}) copy-start(bf16[288,384]{1,0:T(8,128)(2,1)} %param.6) | copy-start | bytes 663556
  603.9 27.8 %collective-permute-start = (bf16[96,384]{1,0:T(8,128)(2,1)S(1)}, bf16[96,384]{1,0:T(8,128)(2,1)S(1)}, u32[]{:S(2)}, u32[]{:S(2)}) collective-permute-start(bf16[96,384]{1,0:T(8,128)(2,1)S(1)} %fusion), channel_id=1, source_target_pairs={{0,1},{1,2},{2,3},{3,4},{4,5},{5,6},{6,7},{7,8},{8,9},{9,10},{10,1... | collective-permute-start | bytes 221192
  607.5 24.3 %collective-permute-start.1 = (bf16[96,384]{1,0:T(8,128)(2,1)S(1)}, bf16[96,384]{1,0:T(8,128)(2,1)S(1)}, u32[]{:S(2)}, u32[]{:S(2)}) collective-permute-start(bf16[96,384]{1,0:T(8,128)(2,1)S(1)} %fusion), channel_id=1, source_target_pairs={{0,2},{1,3},{2,4},{3,5},{4,6},{5,7},{6,8},{7,9},{8,10},{9,11},{10,... | collective-permute-start | bytes 221192
  608.8 23.0 %collective-permute-start.2 = (bf16[96,384]{1,0:T(8,128)(2,1)S(1)}, bf16[96,384]{1,0:T(8,128)(2,1)S(1)}, u32[]{:S(2)}, u32[]{:S(2)}) collective-permute-start(bf16[96,384]{1,0:T(8,128)(2,1)S(1)} %fusion), channel_id=1, source_target_pairs={{0,3},{1,4},{2,5},{3,6},{4,7},{5,8},{6,9},{7,10},{8,11},{9,12},{10... | collective-permute-start | bytes 221192
  610.1 21.7 %collective-permute-start.3 = (bf16[96,384]{1,0:T(8,128)(2,1)S(1)}, bf16[96,384]{1,0:T(8,128)(2,1)S(1)}, u32[]{:S(2)}, u32[]{:S(2)}) collective-permute-start(bf16[96,384]{1,0:T(8,128)(2,1)S(1)} %fusion), channel_id=1, source_target_pairs={{0,4},{1,5},{2,6},{3,7},{4,8},{5,9},{6,10},{7,11},{8,12},{9,13},{1... | collective-permute-start | bytes 221192
  611.4 20.3 %collective-permute-start.4 = (bf16[81,384]{1,0:T(8,128)(2,1)S(1)}, bf16[81,384]{1,0:T(8,128)(2,1)S(1)}, u32[]{:S(2)}, u32[]{:S(2)}) collective-permute-start(bf16[81,384]{1,0:T(8,128)(2,1)S(1)} %slice.16), channel_id=1, source_target_pairs={{0,5},{1,6},{2,7},{3,8},{4,9},{5,10},{6,11},{7,12},{8,13},{9,14},{... | collective-permute-start | bytes 186632
Sparse Core Ops, SparseCore 0:
  13.4 98.1 all-gather.5
  113.7 100.7 all-gather.7
  216.6 82.7 all-gather.9
  301.3 83.2 all-gather.11
where the time goes:
time: 642 us; the launch traced here: 641 us
  waiting for transfers between devices  292 us (45%)
  blocking collectives  154 us (24%)
  local copies, waits for them, and re-layouts  85.7 us (13%)
  other arithmetic  56.5 us (9%)
  starting transfers between devices  28.5 us (4%)
  between operations  14.1 us (2%)
  matrix products  10.2 us (2%)
    all_gather x1, waiting for transfers between devices, local(): selected = lax.all_gather(own_slots, 'ed', axis=1, tiled=True)  96.3 us
    all_gather x1, waiting for transfers between devices, local(): lax.all_gather(w_down[0], 'fsdp', axis=1, tiled=True)  85.3 us
    unnamed x1, blocking collectives  81.8 us
    all_to_all x1, blocking collectives, local(): lax.all_to_all(selected, 'fsdp', split_axis=1, concat_axis=2, tiled=True)  71.7 us
    all_gather x1, waiting for transfers between devices, local(): lax.all_gather(w_up, 'fsdp', axis=1, tiled=True)  66.1 us
    unnamed x2, other arithmetic  50.5 us
    all_to_all x1, waiting for transfers between devices, local(): lax.all_to_all(stacked, 'fsdp', split_axis=2, concat_axis=1, tiled=True)  42.9 us
    unnamed x19, local copies, waits for them, and re-layouts  34.1 us
  transfers between devices with their start and end apart: 10, of which 4 were waited for; matrix products, arithmetic and copies ran while one was open for 8% of the time, Pallas kernels for 0%

commit v1 on v0

--- a/solution.py
+++ b/solution.py
@@ -4,6 +4,12 @@
 from jax.sharding import PartitionSpec as P
 
 CAP = 81
+
+
+def exchange_blocks(shard, axis, split, join):
+    pieces = jnp.split(shard, lax.axis_size(axis), axis=split)
+    arrived = lax.all_to_all(jnp.stack(pieces), axis, 0, 0)
+    return jnp.concatenate(arrived, axis=join)
 
 
 def slot_match(routes, window, capacity):
@@ -74,7 +80,7 @@
     whole_rows = columns_out(lax.all_gather(w_down[0], "fsdp", axis=1, tiled=True), jnp.int32(0))
     outputs_list = [whole_rows.astype(jnp.bfloat16)]
     stacked = jnp.stack(outputs_list)
-    exchanged = lax.all_to_all(stacked, "fsdp", split_axis=2, concat_axis=1, tiled=True)
+    exchanged = exchange_blocks(stacked, "fsdp", 2, 1)
     partial_out = exchanged.astype(jnp.float32)
     slot_out = lax.psum_scatter(
         partial_out.astype(jnp.bfloat16), "ed", scatter_dimension=1, tiled=True

time: 642 us -> 586 us (0.913)
  other arithmetic: 56.5 us -> 21.9 us
  local copies, waits for them, and re-layouts: 85.7 us -> 63.2 us
    unnamed x2 -> x1, other arithmetic: 50.5 us -> 15.8 us
    all_to_all x4 -> x0, local copies, waits for them, and re-layouts: 16 us -> none  [local(): lax.all_to_all(stacked, 'fsdp', split_axis=2, concat_axis=1, tiled=True)]
    another operation x5, local copies, waits for them, and re-layouts: 13.8 us -> 1.68 us  [the longest x1 1.57 us: exchange_blocks(): arrived = lax.all_to_all(jnp.stack(pieces), axis, 0, 0)]
    unnamed x19 -> x29, local copies, waits for them, and re-layouts: 34.1 us -> 38.1 us
  transfers between devices with their start and end apart: 10 -> 10, of which waited for: 4 -> 4; matrix products, arithmetic and copies ran while one was open for 8% -> 9% of each run, Pallas kernels for 0% -> 0%
where the time goes in v1:
time: 586 us; the launch traced here: 585 us
  waiting for transfers between devices  294 us (50%)
  blocking collectives  154 us (26%)
  local copies, waits for them, and re-layouts  63.2 us (11%)
  starting transfers between devices  28.3 us (5%)
  other arithmetic  21.9 us (4%)
  between operations  14 us (2%)
  matrix products  10.3 us (2%)
    all_gather x1, waiting for transfers between devices, local(): selected = lax.all_gather(own_slots, 'ed', axis=1, tiled=True)  96.3 us
    all_gather x1, waiting for transfers between devices, local(): lax.all_gather(w_down[0], 'fsdp', axis=1, tiled=True)  85.3 us
    unnamed x1, blocking collectives  82 us
    all_to_all x1, blocking collectives, local(): lax.all_to_all(selected, 'fsdp', split_axis=1, concat_axis=2, tiled=True)  71.7 us
    all_gather x1, waiting for transfers between devices, local(): lax.all_gather(w_up, 'fsdp', axis=1, tiled=True)  66.1 us
    all_to_all x1, waiting for transfers between devices, exchange_blocks(): arrived = lax.all_to_all(jnp.stack(pieces), axis, 0, 0)  44.4 us
    unnamed x29, local copies, waits for them, and re-layouts  38.1 us
    unnamed x5, starting transfers between devices  24 us
  transfers between devices with their start and end apart: 10, of which 4 were waited for; matrix products, arithmetic and copies ran while one was open for 9% of the time, Pallas kernels for 0%

profile of v1, /device:TPU:1, one launch (start us, length us, event | category | flops | bytes accessed | tf_op | source)
XLA Modules:
  0.0 585.3 jit_solution(956691187740175053)
XLA Ops:
  8.1 3.0 convert_reduce_fusion
  15.4 96.3 %all-gather.6.cloned.1.call-done = bf16[1,2592,384]{2,0,1:T(2,128)(2,1)} async-done(((bf16[1,81,384]{2,0,1:T(2,128)(2,1)}), bf16[1,2592,384]{2,0,1:T(2,128)(2,1)}) %all-gather.6.cloned.1.call-update) | async-done | bytes 1990672 | tf_op jit(solution)/shard_map/all_gather | solution.py:60
  112.2 15.8 %reduce.14 = bf16[2592,384]{1,0:T(8,128)(2,1)S(1)} reduce(bf16[2592,1,384]{2,1,0:T(2,128)(2,1)} %bitcast.130, bf16[]{:T(256)} %broadcast.283), dimensions={1}, to_apply=%bitcast.117.reduce_sub_computation | reduce | bytes 3981314
  128.0 1.6 reshape.467
  129.6 71.7 %all_to_all.20 = bf16[16,2,31104]{2,1,0:T(2,128)(2,1)S(1)} all-to-all(bf16[16,2,31104]{2,1,0:T(2,128)(2,1)} %reshape.467), channel_id=1, replica_groups=mesh['fsdp'=16,'ed'=32] {'fsdp'}, dimensions={0} | all-to-all | bytes 3981312 | tf_op jit(solution)/shard_map/all_to_all | solution.py:61
  201.2 8.9 %reshape.468 = bf16[2592,1,384]{2,1,0:T(2,128)(2,1)} reshape(bf16[16,2,31104]{2,1,0:T(2,128)(2,1)S(1)} %all_to_all.20) | data formatting | bytes 3981312
  210.2 17.6 %bitcast_reduce_fusion = bf16[2592,384]{1,0:T(8,128)(2,1)} fusion(bf16[2592,1,384]{2,1,0:T(2,128)(2,1)} %reshape.468), kind=kLoop, calls=%fused_computation.77 | loop fusion | bytes 3981312 | tf_op jit(solution)/shard_map/all_to_all | solution.py:61
  227.8 1.8 all_to_all.15
  230.6 2.7 fusion.5
  233.3 66.1 %all-gather.10.cloned.1.call-done = bf16[1,6144,256]{2,1,0:T(8,128)(2,1)} async-done(((bf16[1,384,256]{2,1,0:T(8,128)(2,1)}), bf16[1,6144,256]{2,1,0:T(8,128)(2,1)}) %all-gather.10.cloned.1.call-update) | async-done | bytes 3145744 | tf_op jit(solution)/shard_map/all_gather | solution.py:71
  299.3 85.3 %all-gather.12.cloned.1.call-done = bf16[1,256,6144]{2,1,0:T(8,128)(2,1)} async-done(((bf16[1,256,384]{2,1,0:T(8,128)(2,1)}), bf16[1,256,6144]{2,1,0:T(8,128)(2,1)}) %all-gather.12.cloned.1.call-update) | async-done | bytes 3145744 | tf_op jit(solution)/shard_map/all_gather | solution.py:80
  384.6 6.6 %fusion.1 = bf16[1,162,6144]{2,1,0:T(8,128)(2,1)} fusion(bf16[1,256,6144]{2,1,0:T(8,128)(2,1)} %all-gather.12.cloned.1.call-done, bf16[162,6144]{1,0:T(8,128)(2,1)S(1)} %bitcast.126, bf16[1,6144,256]{2,1,0:T(8,128)(2,1)} %all-gather.10.cloned.1.call-done, f32[162,256]{1,0:T(8,128)S(1)} %fusion.5), kind=kOutput, calls=%fused_computation.2 | convolution fusion | flops 1020460032 | bytes 10438656 | tf_op jit(solution)/shard_map/dot_general | solution.py:78
  391.2 1.6 fusion.35
  392.8 1.6 fusion.34
  394.3 1.6 fusion.33
  395.9 1.6 fusion.32
  399.0 1.6 fusion.30
  400.6 1.6 fusion.29
  402.1 1.6 fusion.28
  403.7 1.6 fusion.27
  406.8 1.6 fusion.25
  408.4 1.6 fusion.24
  411.5 1.6 fusion.22
  413.1 1.6 fusion.21
  414.7 1.6 fusion.20
  416.3 4.2 all-to-all-start.1
  420.5 44.4 %all-to-all-done.1 = bf16[16,1,162,384]{3,2,1,0:T(8,128)(2,1)S(1)} async-done(((bf16[16,1,162,384]{3,2,1,0:T(8,128)(2,1)}), bf16[16,1,162,384]{3,2,1,0:T(8,128)(2,1)S(1)}, u32[]{:S(2)}, u32[]{:S(2)}) %all-to-all-start.1) | async-done | bytes 1990688 | tf_op jit(solution)/shard_map/all_to_all | solution.py:11
  466.4 82.0 %fusion = bf16[96,384]{1,0:T(8,128)(2,1)S(1)} fusion(bf16[1,2592,384]{2,1,0:T(8,128)(2,1)} %reshape.448), kind=kCustom, calls=%all-reduce-scatter | all-reduce-scatter fusion | flops 1179649 | bytes 2066432
  548.5 3.4 collective-permute-start
  555.8 16.7 %collective-permute-start.4 = (bf16[81,384]{1,0:T(8,128)(2,1)S(1)}, bf16[81,384]{1,0:T(8,128)(2,1)S(1)}, u32[]{:S(2)}, u32[]{:S(2)}) collective-permute-start(bf16[81,384]{1,0:T(8,128)(2,1)S(1)} %slice.16), channel_id=1, source_target_pairs={{0,5},{1,6},{2,7},{3,8},{4,9},{5,10},{6,11},{7,12},{8,13},{9,14},{... | collective-permute-start | bytes 186632
  572.5 1.7 convert_multiply_fusion
  576.2 1.6 concatenate.3
  (53 shorter events, 19.8 us)
Async XLA Ops:
  6.5 4.6 copy-start
  6.5 105.1 %all-gather.6.cloned.1.call-start = ((), (), s32[]{:S(2)}) async-start(), calls=%async_computation.2 | async-start | bytes 4105728 | tf_op jit(solution)/shard_map/all_gather | solution.py:60
  13.3 217.3 %all-gather.8.cloned.1.call-start = ((), (), s32[]{:S(2)}) async-start(), calls=%async_computation.3 | async-start | bytes 3342336 | tf_op jit(solution)/shard_map/all_gather | solution.py:65
  14.1 285.3 %all-gather.10.cloned.1.call-start = ((), (), s32[]{:S(2)}) async-start(), calls=%async_computation.4 | async-start | bytes 3342336 | tf_op jit(solution)/shard_map/all_gather | solution.py:71
  14.8 369.8 %all-gather.12.cloned.1.call-start = ((), (), s32[]{:S(2)}) async-start(), calls=%async_computation.5 | async-start | bytes 3342336 | tf_op jit(solution)/shard_map/all_gather | solution.py:80
  416.3 4.2 copy-start.1
  416.3 4.2 copy-start.2
  416.3 48.6 %all-to-all-start.1 = ((bf16[16,1,162,384]{3,2,1,0:T(8,128)(2,1)}), bf16[16,1,162,384]{3,2,1,0:T(8,128)(2,1)S(1)}, u32[]{:S(2)}, u32[]{:S(2)}) async-start(bf16[16,1,162,384]{3,2,1,0:T(8,128)(2,1)} %fusion.20), calls=%async_computation.1 | async-start | bytes 4128768 | tf_op jit(solution)/shard_map/all_to_all | solution.py:11
  548.5 27.7 %collective-permute-start = (bf16[96,384]{1,0:T(8,128)(2,1)S(1)}, bf16[96,384]{1,0:T(8,128)(2,1)S(1)}, u32[]{:S(2)}, u32[]{:S(2)}) collective-permute-start(bf16[96,384]{1,0:T(8,128)(2,1)S(1)} %fusion), channel_id=1, source_target_pairs={{0,1},{1,2},{2,3},{3,4},{4,5},{5,6},{6,7},{7,8},{8,9},{9,10},{10,1... | collective-permute-start | bytes 221192
  551.9 24.2 %collective-permute-start.1 = (bf16[96,384]{1,0:T(8,128)(2,1)S(1)}, bf16[96,384]{1,0:T(8,128)(2,1)S(1)}, u32[]{:S(2)}, u32[]{:S(2)}) collective-permute-start(bf16[96,384]{1,0:T(8,128)(2,1)S(1)} %fusion), channel_id=1, source_target_pairs={{0,2},{1,3},{2,4},{3,5},{4,6},{5,7},{6,8},{7,9},{8,10},{9,11},{10,... | collective-permute-start | bytes 221192
  553.2 22.9 %collective-permute-start.2 = (bf16[96,384]{1,0:T(8,128)(2,1)S(1)}, bf16[96,384]{1,0:T(8,128)(2,1)S(1)}, u32[]{:S(2)}, u32[]{:S(2)}) collective-permute-start(bf16[96,384]{1,0:T(8,128)(2,1)S(1)} %fusion), channel_id=1, source_target_pairs={{0,3},{1,4},{2,5},{3,6},{4,7},{5,8},{6,9},{7,10},{8,11},{9,12},{10... | collective-permute-start | bytes 221192
  554.5 21.6 %collective-permute-start.3 = (bf16[96,384]{1,0:T(8,128)(2,1)S(1)}, bf16[96,384]{1,0:T(8,128)(2,1)S(1)}, u32[]{:S(2)}, u32[]{:S(2)}) collective-permute-start(bf16[96,384]{1,0:T(8,128)(2,1)S(1)} %fusion), channel_id=1, source_target_pairs={{0,4},{1,5},{2,6},{3,7},{4,8},{5,9},{6,10},{7,11},{8,12},{9,13},{1... | collective-permute-start | bytes 221192
  555.8 20.3 %collective-permute-start.4 = (bf16[81,384]{1,0:T(8,128)(2,1)S(1)}, bf16[81,384]{1,0:T(8,128)(2,1)S(1)}, u32[]{:S(2)}, u32[]{:S(2)}) collective-permute-start(bf16[81,384]{1,0:T(8,128)(2,1)S(1)} %slice.16), channel_id=1, source_target_pairs={{0,5},{1,6},{2,7},{3,8},{4,9},{5,10},{6,11},{7,12},{8,13},{9,14},{... | collective-permute-start | bytes 186632
Sparse Core Ops, SparseCore 0:
  13.4 98.1 all-gather.5
  113.7 100.7 all-gather.7
  216.6 82.7 all-gather.9
  301.3 83.2 all-gather.11
